TPU v7x, 32 devices: a whole 2x2x4 slice. The times are simulated.
32 devices in a mesh: row: 8 (over y, x, core), col: 4 (over z).
Axes of the slice: x: 2, y: 2, z: 4, core: 2. Of those that a mesh axis runs over, the one named last changes fastest.
Arguments:
- pair: bfloat16 [384, 384, 128], P('row', 'col'), may hold values from -6 to 6
- token_mask: int32 [384], replicated, may hold values from 0 to 1, as said below
- gain: float32 [2, 128], replicated, may hold values from 0.25 to 1.75
- w_proj: bfloat16 [2, 128, 512], replicated, may hold values from -3 to 3
- w_bias: bfloat16 [2, 128, 4], replicated, may hold values from -0.5 to 0.5
- w_out: bfloat16 [2, 128, 128], replicated, may hold values from -0.5 to 0.5
Outputs:
- updated: bfloat16 [384, 384, 128], P('row', 'col')
Inputs may be any that keep to these rules, and one draw needn't show every extreme that they name: `token_mask`: the tokens form 4 chains of 96 positions each; in each chain the first L positions are 1 and the rest 0, with 48 <= L < 96.
All inputs are finite; a program needn't handle non-finite values.
Results may differ from a plain program's by a relative error of at most 0.03.
The roundings to bfloat16 on the way count: a program that leaves them out, or rounds other values in their place, can miss the bound.
Values may be sent and summed in bfloat16 or wider, within the bound.
A program may use at most 128 MiB of HBM per device.

v0:
```python
import math
import jax
import jax.numpy as jnp
from jax import lax
from jax.sharding import PartitionSpec as P

HEADS = 4
HEAD_DIM = 32


def normalize(tile, gain):
    values = tile.astype(jnp.float32)
    average = jnp.mean(values, axis=-1, keepdims=True)
    centred = values - average
    variance = jnp.mean(centred * centred, axis=-1, keepdims=True)
    return (centred * lax.rsqrt(variance + 1e-05) * gain).astype(jnp.bfloat16)


def project(normed, w_proj, w_bias):
    row_count, col_count, channels = normed.shape
    inner = HEADS * HEAD_DIM
    flattened = normed.reshape(row_count * col_count, channels)
    projected = jnp.dot(flattened, w_proj, preferred_element_type=jnp.float32)
    queries = (projected[:, :inner] / jnp.sqrt(jnp.float32(HEAD_DIM))).astype(jnp.bfloat16)
    queries = queries.reshape(row_count, col_count, HEADS, HEAD_DIM)
    key_part = (
        projected[:, inner : 2 * inner].astype(jnp.bfloat16).reshape(row_count, col_count, inner)
    )
    value_part = (
        projected[:, 2 * inner : 3 * inner]
        .astype(jnp.bfloat16)
        .reshape(row_count, col_count, inner)
    )
    gate_part = jax.nn.sigmoid(projected[:, 3 * inner :])
    bias_part = jnp.dot(flattened, w_bias, preferred_element_type=jnp.float32).astype(jnp.bfloat16)
    return (
        queries,
        key_part,
        value_part,
        gate_part,
        bias_part.reshape(row_count, col_count, HEADS),
    )


def keys_from_pairs(normed_piece, w_proj):
    inner = HEADS * HEAD_DIM
    lead = normed_piece.shape[:2]
    flattened = normed_piece.reshape(lead[0] * lead[1], normed_piece.shape[2])
    projected = jnp.dot(flattened, w_proj[:, inner : 3 * inner], preferred_element_type=jnp.float32)
    key_piece = projected[:, :inner].astype(jnp.bfloat16).reshape(lead + (inner,))
    value_piece = projected[:, inner:].astype(jnp.bfloat16).reshape(lead + (inner,))
    return (key_piece, value_piece)


def accumulate(carried, scores, value_piece, form):
    running_max, running_sum, running_acc = carried
    new_max = jnp.maximum(running_max, jnp.max(scores, axis=-1))
    factor = jnp.exp(running_max - new_max)
    weights = jnp.exp(scores - new_max[..., None])
    running_sum = running_sum * factor + jnp.sum(weights, axis=-1)
    product = jnp.einsum(
        form, weights.astype(jnp.bfloat16), value_piece, preferred_element_type=jnp.float32
    )
    return (new_max, running_sum, running_acc * factor[..., None] + product)


def attend_ending(carried, key_piece, value_piece, offset, queries, bias_end, token_mask):
    count = key_piece.shape[0]
    col_count = queries.shape[1]
    key_four = key_piece.reshape(count, col_count, HEADS, HEAD_DIM)
    value_four = value_piece.reshape(count, col_count, HEADS, HEAD_DIM)
    scores = jnp.einsum("ijhd,kjhd->ijhk", queries, key_four, preferred_element_type=jnp.float32)
    bias_slice = lax.dynamic_slice_in_dim(bias_end, offset, count, 0)
    scores = scores + jnp.transpose(bias_slice, (1, 2, 0)).astype(jnp.float32)[:, None]
    live = lax.dynamic_slice_in_dim(token_mask, offset, count, 0)
    scores = jnp.where(live > 0, scores, -1000000000.0)
    return accumulate(carried, scores, value_four, "ijhk,kjhd->ijhd")


def attend_starting(carried, key_piece, value_piece, offset, queries, bias_start, token_mask):
    count = key_piece.shape[1]
    row_count = queries.shape[0]
    key_four = key_piece.reshape(row_count, count, HEADS, HEAD_DIM)
    value_four = value_piece.reshape(row_count, count, HEADS, HEAD_DIM)
    scores = jnp.einsum("ijhd,ikhd->ijhk", queries, key_four, preferred_element_type=jnp.float32)
    bias_slice = lax.dynamic_slice_in_dim(bias_start, offset, count, 1)
    scores = scores + jnp.transpose(bias_slice, (0, 2, 1)).astype(jnp.float32)[None]
    live = lax.dynamic_slice_in_dim(token_mask, offset, count, 0)
    scores = jnp.where(live > 0, scores, -1000000000.0)
    return accumulate(carried, scores, value_four, "ijhk,ikhd->ijhd")


def fold_blocks(carried, pieces, along, convert, attend):
    count = pieces[0].shape[along]
    width = math.gcd(count, 128)

    def one_block(index, carry):
        start = index * width
        blocks = tuple((lax.dynamic_slice_in_dim(piece, start, width, along) for piece in pieces))
        key_block, value_block = convert(blocks)
        return attend(carry, key_block, value_block, start)

    return lax.fori_loop(0, count // width, one_block, carried)


def select_bias(bias_part, row_count, col_count, ending):
    bias_rowwise = lax.all_gather(bias_part, "row", axis=0, tiled=True)
    full_bias = lax.all_gather(bias_rowwise, "col", axis=1, tiled=True)
    if ending:
        return lax.dynamic_slice_in_dim(full_bias, lax.axis_index("row") * row_count, row_count, 1)
    return lax.dynamic_slice_in_dim(full_bias, lax.axis_index("col") * col_count, col_count, 0)


def run_pass(tile, token_mask, gain, w_proj, w_bias, w_out, ending):
    row_count, col_count, channels = tile.shape
    normed = normalize(tile, gain)
    queries, key_part, value_part, gate_part, bias_part = project(normed, w_proj, w_bias)
    bias_local = select_bias(bias_part, row_count, col_count, ending)
    start_max = jnp.full((row_count, col_count, HEADS), -1e30, jnp.float32)
    start_sum = jnp.zeros((row_count, col_count, HEADS), jnp.float32)
    start_acc = jnp.zeros((row_count, col_count, HEADS, HEAD_DIM), jnp.float32)
    initial = (start_max, start_sum, start_acc)

    def project_pairs(blocks):
        return keys_from_pairs(blocks[0], w_proj)

    if ending:

        def ending_step(carry, key_block, value_block, position):
            return attend_ending(
                carry, key_block, value_block, position, queries, bias_local, token_mask
            )

        def fold_pairs(carried, received, offset):
            return fold_blocks(carried, (received,), 0, project_pairs, ending_step)

        result = fold_pairs(
            initial, lax.all_gather(normed, "row", axis=0, tiled=True), jnp.int32(0)
        )
    else:

        def starting_step(carry, key_block, value_block, position):
            return attend_starting(
                carry, key_block, value_block, position, queries, bias_local, token_mask
            )

        def fold_pairs(carried, received, offset):
            return fold_blocks(carried, (received,), 1, project_pairs, starting_step)

        result = fold_pairs(
            initial, lax.all_gather(normed, "col", axis=1, tiled=True), jnp.int32(0)
        )
    final_max, final_sum, final_acc = result
    attended = final_acc / final_sum[..., None]
    gated = (gate_part * attended.reshape(row_count * col_count, HEADS * HEAD_DIM)).astype(
        jnp.bfloat16
    )
    update = jnp.dot(gated, w_out, preferred_element_type=jnp.float32)
    return (tile.astype(jnp.float32) + update.reshape(row_count, col_count, channels)).astype(
        jnp.bfloat16
    )


def local(pair, token_mask, gain, w_proj, w_bias, w_out):
    first = run_pass(pair, token_mask, gain[0], w_proj[0], w_bias[0], w_out[0], True)
    return run_pass(first, token_mask, gain[1], w_proj[1], w_bias[1], w_out[1], False)


def solution(mesh):
    return jax.shard_map(
        local,
        mesh=mesh,
        in_specs=(P("row", "col", None), P(), P(), P(), P(), P()),
        out_specs=P("row", "col", None),
        check_vma=False,
    )
```

profile of v0, /device:TPU:0, one launch (start us, length us, event | category | flops | bytes accessed | tf_op | source)
XLA Modules:
  0.0 606.3 jit_solution(17036669407147317621)
XLA Ops:
  13.7 11.1 %all_gather.19 = bf16[384,96,4]{1,2,0:T(4,128)(2,1)S(1)} all-gather(bf16[48,96,4]{1,2,0:T(4,128)(2,1)S(1)} %copy.62), channel_id=1, replica_groups=mesh['row'=8,'col'=4] {'row'}, dimensions={0}, use_global_device_ids=true | all-gather | bytes 331776 | tf_op jit(solution)/shard_map/all_gather | solution.py:107
  29.3 3.7 copy-done.3
  35.4 5.2 copy.64
  41.4 15.1 %all-gather.7.cloned.1.call-done = bf16[384,384,4]{0,2,1:T(4,128)(2,1)} async-done(((bf16[384,96,4]{0,2,1:T(4,128)(2,1)}), bf16[384,384,4]{0,2,1:T(4,128)(2,1)}) %all-gather.7.cloned.1.call-update) | async-done | bytes 1179664 | tf_op jit(solution)/shard_map/all_gather | solution.py:108
  58.1 58.2 %all-gather.5.cloned.1.call-done = bf16[384,96,128]{2,1,0:T(8,128)(2,1)} async-done(((bf16[48,96,128]{2,1,0:T(8,128)(2,1)}), bf16[384,96,128]{2,1,0:T(8,128)(2,1)}) %all-gather.5.cloned.1.call-update) | async-done | bytes 9437200 | tf_op jit(solution)/shard_map/all_gather | solution.py:138
  116.3 207.9 %while.36 = (s32[]{:T(128)}, f32[48,96,4]{0,2,1:T(4,128)}, f32[48,96,4]{0,2,1:T(4,128)}, f32[48,96,4,32]{0,3,2,1:T(8,128)}, s32[384]{0:T(512)S(1)}, /*index=5*/b...) while((s32[]{:T(128)}, f32[48,96,4]{0,2,1:T(4,128)}, ...), condition=%wide.region_5.6_spmd.clone, body=%wide.region_2.5_spmd.clone.sunk | while | flops 1138280576 | bytes 109233432 | solution.py:103
  124.5 3.2 copy.97
  127.7 5.2 reshape.122
  132.9 6.1 %copy.98 = bf16[128,96,4,32]{0,3,2,1:T(8,128)(2,1)S(1)} copy(bf16[128,96,4,32]{1,0,3,2:T(8,128)(2,1)} %reshape.122) | data formatting | bytes 6291456 | tf_op jit(solution)/shard_map/while/body/eval_jaxpr/reshape;while/body/eval_jaxpr/reshape | solution.py:70
  139.9 10.1 %fusion.107 = (f32[48,96,4]{0,2,1:T(4,128)}, f32[96,4,128,48]{2,3,1,0:T(8,128)}) fusion(f32[48,4,128]{2,0,1:T(8,128)S(1)} %convert_bitcast_fusion.4, pred[128]{0:T(512)(128)(4,1)S(1)} %dynamic-slice_compare_fusion.4, bf16[128,96,4,32]{0,3,2,1:T(8,128)(2,1)S(1)} %copy.98, bf16[48,96,4,32]{0,3,2,1:T(8,128)(2,1)} %get-tuple-element.672), kind=kOutput, calls=%fused_computation.6.clone.1 | convolution fusion | flops 158054400 | bytes 13934720 | tf_op jit(solution)/shard_map/while/body/eval_jaxpr/ijhd,kjhd->ijhk/dot_general | solution.py:72
  151.1 8.3 %fusion.108 = f32[48,96,4]{0,2,1:T(4,128)S(1)} fusion(f32[96,4,128,48]{2,3,1,0:T(8,128)} %get-tuple-element.620, f32[48,96,4]{0,2,1:T(4,128)S(1)} %select_maximum_fusion.4, f32[48,4,128]{2,0,1:T(8,128)S(1)} %convert_bitcast_fusion.4, pred[128]{0:T(512)(128)(4,1)S(1)} %dynamic-slice_compare_fusion.4), kind=kLoop, calls=%fused_computation.5.clone.1 | loop fusion | flops 9418752 | bytes 9683072 | tf_op jit(solution)/shard_map/while/body/eval_jaxpr/reduce_sum | solution.py:60
  161.0 3.2 copy.99
  164.2 5.2 reshape.123
  169.4 6.1 %copy.100 = bf16[128,96,4,32]{0,3,2,1:T(8,128)(2,1)S(1)} copy(bf16[128,96,4,32]{1,0,3,2:T(8,128)(2,1)} %reshape.123) | data formatting | bytes 6291456 | tf_op jit(solution)/shard_map/while/body/eval_jaxpr/reshape;while/body/eval_jaxpr/reshape | solution.py:71
  175.5 8.7 %bitcast_add_fusion.6 = f32[48,96,4,32]{0,3,2,1:T(8,128)} fusion(f32[48,96,4,32]{0,3,2,1:T(8,128)} %get-tuple-element.655, f32[48,96,4]{0,2,1:T(4,128)} %get-tuple-element.622, pred[]{:T(512)S(6)} %compare.6, bf16[128,96,4,32]{0,3,2,1:T(8,128)(2,1)S(1)} %copy.100, f32[96,4,128,48]{2,3,1,0:T(8,128)} %get-tuple-element.620, ...), kind=kOutput, calls=%fused_computation.7.clone.1 | convolution fusion | flops 162201600 | bytes 17547392 | tf_op jit(solution)/shard_map/while/body/eval_jaxpr/ijhk,kjhd->ijhd/dot_general | solution.py:61
  192.6 3.2 copy.97
  195.8 5.2 reshape.122
  201.0 6.1 %copy.98 = bf16[128,96,4,32]{0,3,2,1:T(8,128)(2,1)S(1)} copy(bf16[128,96,4,32]{1,0,3,2:T(8,128)(2,1)} %reshape.122) | data formatting | bytes 6291456 | tf_op jit(solution)/shard_map/while/body/eval_jaxpr/reshape;while/body/eval_jaxpr/reshape | solution.py:70
  208.0 10.1 %fusion.107 = (f32[48,96,4]{0,2,1:T(4,128)}, f32[96,4,128,48]{2,3,1,0:T(8,128)}) fusion(f32[48,4,128]{2,0,1:T(8,128)S(1)} %convert_bitcast_fusion.4, pred[128]{0:T(512)(128)(4,1)S(1)} %dynamic-slice_compare_fusion.4, bf16[128,96,4,32]{0,3,2,1:T(8,128)(2,1)S(1)} %copy.98, bf16[48,96,4,32]{0,3,2,1:T(8,128)(2,1)} %get-tuple-element.672), kind=kOutput, calls=%fused_computation.6.clone.1 | convolution fusion | flops 158054400 | bytes 13934720 | tf_op jit(solution)/shard_map/while/body/eval_jaxpr/ijhd,kjhd->ijhk/dot_general | solution.py:72
  219.3 8.3 %fusion.108 = f32[48,96,4]{0,2,1:T(4,128)S(1)} fusion(f32[96,4,128,48]{2,3,1,0:T(8,128)} %get-tuple-element.620, f32[48,96,4]{0,2,1:T(4,128)S(1)} %select_maximum_fusion.4, f32[48,4,128]{2,0,1:T(8,128)S(1)} %convert_bitcast_fusion.4, pred[128]{0:T(512)(128)(4,1)S(1)} %dynamic-slice_compare_fusion.4), kind=kLoop, calls=%fused_computation.5.clone.1 | loop fusion | flops 9418752 | bytes 9683072 | tf_op jit(solution)/shard_map/while/body/eval_jaxpr/reduce_sum | solution.py:60
  229.2 3.2 copy.99
  232.4 5.2 reshape.123
  237.6 6.1 %copy.100 = bf16[128,96,4,32]{0,3,2,1:T(8,128)(2,1)S(1)} copy(bf16[128,96,4,32]{1,0,3,2:T(8,128)(2,1)} %reshape.123) | data formatting | bytes 6291456 | tf_op jit(solution)/shard_map/while/body/eval_jaxpr/reshape;while/body/eval_jaxpr/reshape | solution.py:71
  243.7 10.1 %bitcast_add_fusion.6 = f32[48,96,4,32]{0,3,2,1:T(8,128)} fusion(f32[48,96,4,32]{0,3,2,1:T(8,128)} %get-tuple-element.655, f32[48,96,4]{0,2,1:T(4,128)} %get-tuple-element.622, pred[]{:T(512)S(6)} %compare.6, bf16[128,96,4,32]{0,3,2,1:T(8,128)(2,1)S(1)} %copy.100, f32[96,4,128,48]{2,3,1,0:T(8,128)} %get-tuple-element.620, ...), kind=kOutput, calls=%fused_computation.7.clone.1 | convolution fusion | flops 162201600 | bytes 17547392 | tf_op jit(solution)/shard_map/while/body/eval_jaxpr/ijhk,kjhd->ijhd/dot_general | solution.py:61
  262.3 3.2 copy.97
  265.4 5.2 reshape.122
  270.6 6.1 %copy.98 = bf16[128,96,4,32]{0,3,2,1:T(8,128)(2,1)S(1)} copy(bf16[128,96,4,32]{1,0,3,2:T(8,128)(2,1)} %reshape.122) | data formatting | bytes 6291456 | tf_op jit(solution)/shard_map/while/body/eval_jaxpr/reshape;while/body/eval_jaxpr/reshape | solution.py:70
  277.6 10.1 %fusion.107 = (f32[48,96,4]{0,2,1:T(4,128)}, f32[96,4,128,48]{2,3,1,0:T(8,128)}) fusion(f32[48,4,128]{2,0,1:T(8,128)S(1)} %convert_bitcast_fusion.4, pred[128]{0:T(512)(128)(4,1)S(1)} %dynamic-slice_compare_fusion.4, bf16[128,96,4,32]{0,3,2,1:T(8,128)(2,1)S(1)} %copy.98, bf16[48,96,4,32]{0,3,2,1:T(8,128)(2,1)} %get-tuple-element.672), kind=kOutput, calls=%fused_computation.6.clone.1 | convolution fusion | flops 158054400 | bytes 13934720 | tf_op jit(solution)/shard_map/while/body/eval_jaxpr/ijhd,kjhd->ijhk/dot_general | solution.py:72
  288.9 8.3 %fusion.108 = f32[48,96,4]{0,2,1:T(4,128)S(1)} fusion(f32[96,4,128,48]{2,3,1,0:T(8,128)} %get-tuple-element.620, f32[48,96,4]{0,2,1:T(4,128)S(1)} %select_maximum_fusion.4, f32[48,4,128]{2,0,1:T(8,128)S(1)} %convert_bitcast_fusion.4, pred[128]{0:T(512)(128)(4,1)S(1)} %dynamic-slice_compare_fusion.4), kind=kLoop, calls=%fused_computation.5.clone.1 | loop fusion | flops 9418752 | bytes 9683072 | tf_op jit(solution)/shard_map/while/body/eval_jaxpr/reduce_sum | solution.py:60
  302.0 5.2 reshape.123
  307.2 6.1 %copy.100 = bf16[128,96,4,32]{0,3,2,1:T(8,128)(2,1)S(1)} copy(bf16[128,96,4,32]{1,0,3,2:T(8,128)(2,1)} %reshape.123) | data formatting | bytes 6291456 | tf_op jit(solution)/shard_map/while/body/eval_jaxpr/reshape;while/body/eval_jaxpr/reshape | solution.py:71
  313.3 10.1 %bitcast_add_fusion.6 = f32[48,96,4,32]{0,3,2,1:T(8,128)} fusion(f32[48,96,4,32]{0,3,2,1:T(8,128)} %get-tuple-element.655, f32[48,96,4]{0,2,1:T(4,128)} %get-tuple-element.622, pred[]{:T(512)S(6)} %compare.6, bf16[128,96,4,32]{0,3,2,1:T(8,128)(2,1)S(1)} %copy.100, f32[96,4,128,48]{2,3,1,0:T(8,128)} %get-tuple-element.620, ...), kind=kOutput, calls=%fused_computation.7.clone.1 | convolution fusion | flops 162201600 | bytes 17547392 | tf_op jit(solution)/shard_map/while/body/eval_jaxpr/ijhk,kjhd->ijhd/dot_general | solution.py:61
  324.2 6.9 %broadcast_divide_fusion = f32[48,96,4,32]{0,3,2,1:T(8,128)} fusion(f32[48,96,4,32]{0,3,2,1:T(8,128)} %get-tuple-element.315, f32[48,96,4]{0,2,1:T(4,128)} %get-tuple-element.316), kind=kLoop, calls=%fused_computation.58 | loop fusion | flops 589824 | bytes 4792320 | tf_op jit(solution)/shard_map/div | solution.py:154
  331.1 5.4 copy.66
  348.5 9.5 %all_gather.22 = bf16[384,96,4]{1,2,0:T(4,128)(2,1)S(1)} all-gather(bf16[48,96,4]{1,2,0:T(4,128)(2,1)S(1)} %copy.69), channel_id=1, replica_groups=mesh['row'=8,'col'=4] {'row'}, dimensions={0}, use_global_device_ids=true | all-gather | bytes 331776 | tf_op jit(solution)/shard_map/all_gather | solution.py:107
  362.3 3.7 copy-done.4
  370.3 19.2 %all-gather.11.cloned.1.call-done = bf16[384,384,4]{0,2,1:T(4,128)(2,1)} async-done(((bf16[384,96,4]{0,2,1:T(4,128)(2,1)}), bf16[384,384,4]{0,2,1:T(4,128)(2,1)}) %all-gather.11.cloned.1.call-update) | async-done | bytes 1179664 | tf_op jit(solution)/shard_map/all_gather | solution.py:108
  391.9 87.7 %all-gather.9.cloned.1.call-done = bf16[48,384,128]{2,1,0:T(8,128)(2,1)} async-done(((bf16[48,96,128]{2,1,0:T(8,128)(2,1)}), bf16[48,384,128]{2,1,0:T(8,128)(2,1)}) %all-gather.9.cloned.1.call-update) | async-done | bytes 4718608 | tf_op jit(solution)/shard_map/all_gather | solution.py:151
  479.5 107.2 %while.37 = (s32[]{:T(128)}, f32[48,96,4]{1,2,0:T(4,128)S(1)}, f32[48,96,4]{1,2,0:T(4,128)}, f32[48,96,4,32]{1,3,2,0:T(8,128)}, s32[384]{0:T(512)S(1)}, /*index=...) while((s32[]{:T(128)}, f32[48,96,4]{1,2,0:T(4,128)S(1)}, ...), condition=%wide.region_11.12_spmd.clone, body=%wide.region_8.11_spmd.clone.sunk | while | flops 734079104 | bytes 90703208 | solution.py:103
  487.4 5.4 fusion.116
  492.9 8.7 %fusion.117 = f32[48,96,4]{1,2,0:T(4,128)S(1)} fusion(f32[48,4,128,96]{2,3,1,0:T(8,128)} %get-tuple-element.635, f32[48,96,4]{1,2,0:T(4,128)S(1)} %select_maximum_fusion.5, f32[96,4,128]{2,0,1:T(8,128)S(1)} %convert_bitcast_fusion.5, pred[128]{0:T(512)(128)(4,1)S(1)} %dynamic-slice_compare_fusion.5), kind=kLoop, calls=%fused_computation.28.clone.1 | loop fusion | flops 9418752 | bytes 9781376 | tf_op jit(solution)/shard_map/while/body/eval_jaxpr/reduce_sum | solution.py:60
  505.0 8.0 %bitcast_add_fusion.7 = f32[48,96,4,32]{1,3,2,0:T(8,128)S(1)} fusion(f32[48,96,4,32]{1,3,2,0:T(8,128)S(1)} %copy-done, f32[48,4,128,96]{2,3,1,0:T(8,128)} %get-tuple-element.635, f32[48,96,4]{1,2,0:T(4,128)S(1)} %select_maximum_fusion.5, f32[96,4,128]{2,0,1:T(8,128)S(1)} %convert_bitcast_fusion.5, ...), kind=kOutput, calls=%fused_computation.36.clone.1 | convolution fusion | flops 162201600 | bytes 16072833 | tf_op jit(solution)/shard_map/while/body/eval_jaxpr/ijhk,ikhd->ijhd/dot_general | solution.py:61
  522.6 5.4 fusion.116
  528.0 8.7 %fusion.117 = f32[48,96,4]{1,2,0:T(4,128)S(1)} fusion(f32[48,4,128,96]{2,3,1,0:T(8,128)} %get-tuple-element.635, f32[48,96,4]{1,2,0:T(4,128)S(1)} %select_maximum_fusion.5, f32[96,4,128]{2,0,1:T(8,128)S(1)} %convert_bitcast_fusion.5, pred[128]{0:T(512)(128)(4,1)S(1)} %dynamic-slice_compare_fusion.5), kind=kLoop, calls=%fused_computation.28.clone.1 | loop fusion | flops 9418752 | bytes 9781376 | tf_op jit(solution)/shard_map/while/body/eval_jaxpr/reduce_sum | solution.py:60
  541.0 8.0 %bitcast_add_fusion.7 = f32[48,96,4,32]{1,3,2,0:T(8,128)S(1)} fusion(f32[48,96,4,32]{1,3,2,0:T(8,128)S(1)} %copy-done, f32[48,4,128,96]{2,3,1,0:T(8,128)} %get-tuple-element.635, f32[48,96,4]{1,2,0:T(4,128)S(1)} %select_maximum_fusion.5, f32[96,4,128]{2,0,1:T(8,128)S(1)} %convert_bitcast_fusion.5, ...), kind=kOutput, calls=%fused_computation.36.clone.1 | convolution fusion | flops 162201600 | bytes 16072833 | tf_op jit(solution)/shard_map/while/body/eval_jaxpr/ijhk,ikhd->ijhd/dot_general | solution.py:61
  558.6 5.4 fusion.116
  564.1 8.7 %fusion.117 = f32[48,96,4]{1,2,0:T(4,128)S(1)} fusion(f32[48,4,128,96]{2,3,1,0:T(8,128)} %get-tuple-element.635, f32[48,96,4]{1,2,0:T(4,128)S(1)} %select_maximum_fusion.5, f32[96,4,128]{2,0,1:T(8,128)S(1)} %convert_bitcast_fusion.5, pred[128]{0:T(512)(128)(4,1)S(1)} %dynamic-slice_compare_fusion.5), kind=kLoop, calls=%fused_computation.28.clone.1 | loop fusion | flops 9418752 | bytes 9781376 | tf_op jit(solution)/shard_map/while/body/eval_jaxpr/reduce_sum | solution.py:60
  577.1 8.0 %bitcast_add_fusion.7 = f32[48,96,4,32]{1,3,2,0:T(8,128)S(1)} fusion(f32[48,96,4,32]{1,3,2,0:T(8,128)S(1)} %copy-done, f32[48,4,128,96]{2,3,1,0:T(8,128)} %get-tuple-element.635, f32[48,96,4]{1,2,0:T(4,128)S(1)} %select_maximum_fusion.5, f32[96,4,128]{2,0,1:T(8,128)S(1)} %convert_bitcast_fusion.5, ...), kind=kOutput, calls=%fused_computation.36.clone.1 | convolution fusion | flops 162201600 | bytes 16072833 | tf_op jit(solution)/shard_map/while/body/eval_jaxpr/ijhk,ikhd->ijhd/dot_general | solution.py:61
  (205 shorter events, 131.7 us)
Async XLA Ops:
  6.5 5.1 copy-start.10
  6.5 4.6 copy-start.24
  6.5 6.6 %copy-start.21 = (bf16[2,128,4]{1,2,0:T(4,128)(2,1)S(1)}, bf16[2,128,4]{1,2,0:T(4,128)(2,1)}, u32[]{:S(2)}) copy-start(bf16[2,128,4]{1,2,0:T(4,128)(2,1)} %param.14) | copy-start | bytes 6148
  6.5 49.9 %all-gather.7.cloned.1.call-start = ((), (), s32[]{:S(2)}) async-start(), calls=%async_computation.1 | async-start | bytes 1474560 | tf_op jit(solution)/shard_map/all_gather | solution.py:108
  13.1 12.7 %copy-start.5 = (bf16[48,96,128]{2,1,0:T(8,128)(2,1)}, bf16[48,96,128]{2,1,0:T(8,128)(2,1)S(1)}, u32[]{:S(2)}) copy-start(bf16[48,96,128]{2,1,0:T(8,128)(2,1)S(1)} %fusion.42) | copy-start | bytes 3538948
  13.1 13.5 %copy-start.17 = (bf16[2,128,512]{2,1,0:T(8,128)(2,1)S(1)}, bf16[2,128,512]{2,1,0:T(8,128)(2,1)}, u32[]{:S(2)}) copy-start(bf16[2,128,512]{2,1,0:T(8,128)(2,1)} %param.13) | copy-start | bytes 786436
  25.8 90.6 %all-gather.5.cloned.1.call-start = ((), (), s32[]{:S(2)}) async-start(), calls=%async_computation | async-start | bytes 10616832 | tf_op jit(solution)/shard_map/all_gather | solution.py:138
  26.5 362.9 %all-gather.11.cloned.1.call-start = ((), (), s32[]{:S(2)}) async-start(), calls=%async_computation.3 | async-start | bytes 1474560 | tf_op jit(solution)/shard_map/all_gather | solution.py:108
  29.3 3.7 copy-start.3
  35.4 80.9 %copy-start.25 = (s32[384]{0:T(512)S(1)}, s32[384]{0:T(512)}, u32[]{:S(2)}) copy-start(s32[384]{0:T(512)} %param.11) | copy-start | bytes 4612
  151.0 8.3 %copy-start.7 = (f32[48,96,4]{0,2,1:T(4,128)S(1)}, f32[48,96,4]{0,2,1:T(4,128)}, u32[]{:S(2)}) copy-start(f32[48,96,4]{0,2,1:T(4,128)} %get-tuple-element.653) | copy-start | bytes 221188 | tf_op jit(solution)/shard_map/while
  151.1 8.3 %copy-start.13 = (f32[48,96,4]{0,2,1:T(4,128)S(1)}, f32[48,96,4]{0,2,1:T(4,128)}, u32[]{:S(2)}) copy-start(f32[48,96,4]{0,2,1:T(4,128)} %get-tuple-element.654) | copy-start | bytes 221188 | tf_op jit(solution)/shard_map/while
  160.3 0.7 copy-start.14
  219.2 8.3 %copy-start.7 = (f32[48,96,4]{0,2,1:T(4,128)S(1)}, f32[48,96,4]{0,2,1:T(4,128)}, u32[]{:S(2)}) copy-start(f32[48,96,4]{0,2,1:T(4,128)} %get-tuple-element.653) | copy-start | bytes 221188 | tf_op jit(solution)/shard_map/while
  219.2 8.3 %copy-start.13 = (f32[48,96,4]{0,2,1:T(4,128)S(1)}, f32[48,96,4]{0,2,1:T(4,128)}, u32[]{:S(2)}) copy-start(f32[48,96,4]{0,2,1:T(4,128)} %get-tuple-element.654) | copy-start | bytes 221188 | tf_op jit(solution)/shard_map/while
  228.5 0.7 copy-start.14
  288.8 8.3 %copy-start.7 = (f32[48,96,4]{0,2,1:T(4,128)S(1)}, f32[48,96,4]{0,2,1:T(4,128)}, u32[]{:S(2)}) copy-start(f32[48,96,4]{0,2,1:T(4,128)} %get-tuple-element.653) | copy-start | bytes 221188 | tf_op jit(solution)/shard_map/while
  288.9 8.3 %copy-start.13 = (f32[48,96,4]{0,2,1:T(4,128)S(1)}, f32[48,96,4]{0,2,1:T(4,128)}, u32[]{:S(2)}) copy-start(f32[48,96,4]{0,2,1:T(4,128)} %get-tuple-element.654) | copy-start | bytes 221188 | tf_op jit(solution)/shard_map/while
  298.1 0.7 copy-start.14
  341.2 2.4 copy-start.11
  341.2 2.4 copy-start.19
  343.7 2.8 copy-start.23
  344.7 1.7 copy-start.8
  344.7 3.2 copy-start.22
  347.9 11.2 %copy-start.6 = (bf16[48,96,128]{2,1,0:T(8,128)(2,1)}, bf16[48,96,128]{2,1,0:T(8,128)(2,1)S(1)}, u32[]{:S(2)}) copy-start(bf16[48,96,128]{2,1,0:T(8,128)(2,1)S(1)} %fusion.39) | copy-start | bytes 3538948
  347.9 11.7 %copy-start.18 = (bf16[2,128,512]{2,1,0:T(8,128)(2,1)S(1)}, bf16[2,128,512]{2,1,0:T(8,128)(2,1)}, u32[]{:S(2)}) copy-start(bf16[2,128,512]{2,1,0:T(8,128)(2,1)} %param.13) | copy-start | bytes 786436
  359.1 120.5 %all-gather.9.cloned.1.call-start = ((), (), s32[]{:S(2)}) async-start(), calls=%async_computation.2 | async-start | bytes 5898240 | tf_op jit(solution)/shard_map/all_gather | solution.py:151
  362.3 3.7 copy-start.4
  479.5 13.3 %copy-start.12 = (f32[48,96,4]{1,2,0:T(4,128)}, f32[48,96,4]{1,2,0:T(4,128)S(1)}, u32[]{:S(2)}) copy-start(f32[48,96,4]{1,2,0:T(4,128)S(1)} %get-tuple-element.692) | copy-start | bytes 221188 | tf_op jit(solution)/shard_map/while
  486.0 1.5 copy-start.2
  492.9 8.7 %copy-start.15 = (f32[48,96,4]{1,2,0:T(4,128)S(1)}, f32[48,96,4]{1,2,0:T(4,128)}, u32[]{:S(2)}) copy-start(f32[48,96,4]{1,2,0:T(4,128)} %get-tuple-element.693) | copy-start | bytes 221188 | tf_op jit(solution)/shard_map/while
  501.8 0.6 copy-start.16
  503.1 1.9 copy-start
  513.0 1.7 copy-start.1
  514.7 13.3 %copy-start.12 = (f32[48,96,4]{1,2,0:T(4,128)}, f32[48,96,4]{1,2,0:T(4,128)S(1)}, u32[]{:S(2)}) copy-start(f32[48,96,4]{1,2,0:T(4,128)S(1)} %get-tuple-element.692) | copy-start | bytes 221188 | tf_op jit(solution)/shard_map/while
  521.1 1.5 copy-start.2
  528.0 8.7 %copy-start.15 = (f32[48,96,4]{1,2,0:T(4,128)S(1)}, f32[48,96,4]{1,2,0:T(4,128)}, u32[]{:S(2)}) copy-start(f32[48,96,4]{1,2,0:T(4,128)} %get-tuple-element.693) | copy-start | bytes 221188 | tf_op jit(solution)/shard_map/while
  537.8 0.6 copy-start.16
  539.2 1.9 copy-start
  549.0 1.7 copy-start.1
  550.7 13.3 %copy-start.12 = (f32[48,96,4]{1,2,0:T(4,128)}, f32[48,96,4]{1,2,0:T(4,128)S(1)}, u32[]{:S(2)}) copy-start(f32[48,96,4]{1,2,0:T(4,128)S(1)} %get-tuple-element.692) | copy-start | bytes 221188 | tf_op jit(solution)/shard_map/while
  557.2 1.5 copy-start.2
  564.1 8.7 %copy-start.15 = (f32[48,96,4]{1,2,0:T(4,128)S(1)}, f32[48,96,4]{1,2,0:T(4,128)}, u32[]{:S(2)}) copy-start(f32[48,96,4]{1,2,0:T(4,128)} %get-tuple-element.693) | copy-start | bytes 221188 | tf_op jit(solution)/shard_map/while
  573.9 0.6 copy-start.16
  575.2 1.9 copy-start
  585.1 1.7 copy-start.1
  595.6 2.4 copy-start.9
  595.6 2.4 copy-start.20
Sparse Core Ops, SparseCore 0:
  25.9 30.5 all-gather.6
  58.4 57.9 all-gather.4
  359.2 30.2 all-gather.10
  390.9 88.6 all-gather.8
where the time goes:
time: 615 us; the launch traced here: 606 us
  local copies, waits for them, and re-layouts  181 us (29%)
  waiting for transfers between devices  181 us (29%)
  matrix products  121 us (20%)
  other arithmetic  86.8 us (14%)
  blocking collectives  20.6 us (3%)
  between operations  13.8 us (2%)
    all_gather x1, waiting for transfers between devices, run_pass(): lax.all_gather(normed, 'col', axis=1, tiled=True)  87.7 us
    all_gather x1, waiting for transfers between devices, run_pass(): lax.all_gather(normed, 'row', axis=0, tiled=True)  58.2 us
    dot_general x6, matrix products, accumulate(): jnp.einsum(form, weights.astype(jnp.bfloat16), value_piece, preferred_ele...  52.8 us
    reduce_sum x6, other arithmetic, accumulate(): running_sum = running_sum * factor + jnp.sum(weights, axis=-1)  51.1 us
    all_gather x2, waiting for transfers between devices, select_bias(): full_bias = lax.all_gather(bias_rowwise, 'col', axis=1, tiled=True)  34.3 us
    reshape x6, local copies, waits for them, and re-layouts, attend_ending(): value_four = value_piece.reshape(count, col_count, HEADS, HEAD_DIM)  33.9 us
    reshape x6, local copies, waits for them, and re-layouts, attend_ending(): key_four = key_piece.reshape(count, col_count, HEADS, HEAD_DIM)  33.8 us
    dot_general x3, matrix products, attend_ending(): jnp.einsum('ijhd,kjhd->ijhk', queries, key_four, preferred_element_type=j...  30.3 us
  transfers between devices with their start and end apart: 4, of which 4 were waited for; matrix products, arithmetic and copies ran while one was open for 4% of the time, Pallas kernels for 0%

commit v1 on v0

--- a/solution.py
+++ b/solution.py
@@ -6,6 +6,13 @@
 
 HEADS = 4
 HEAD_DIM = 32
+
+
+def exchange_gather(array, axis, d):
+    devices = lax.axis_size(axis)
+    shards = jnp.stack([array for _ in range(devices)])
+    shards = lax.all_to_all(shards, axis, split_axis=0, concat_axis=0)
+    return jnp.concatenate(shards, axis=d)
 
 
 def normalize(tile, gain):
@@ -134,9 +141,7 @@
         def fold_pairs(carried, received, offset):
             return fold_blocks(carried, (received,), 0, project_pairs, ending_step)
 
-        result = fold_pairs(
-            initial, lax.all_gather(normed, "row", axis=0, tiled=True), jnp.int32(0)
-        )
+        result = fold_pairs(initial, exchange_gather(normed, "row", 0), jnp.int32(0))
     else:
 
         def starting_step(carry, key_block, value_block, position):

time: 615 us -> 666 us (1.083)
  blocking collectives: 20.6 us -> 119 us
  waiting for transfers between devices: 181 us -> 124 us
    all_gather x2, blocking collectives: 20.6 us -> 119 us  [select_bias(): bias_rowwise = lax.all_gather(bias_part, 'row', axis=0, tiled=True)]
    all_gather x1 -> x0, waiting for transfers between devices: 58.2 us -> none  [run_pass(): lax.all_gather(normed, 'row', axis=0, tiled=True)]
    unnamed x37 -> x35, local copies, waits for them, and re-layouts: 15.2 us -> 15.1 us
  transfers between devices with their start and end apart: 4 -> 4, of which waited for: 4 -> 3; matrix products, arithmetic and copies ran while one was open for 4% -> 3% of each run, Pallas kernels for 0% -> 0%
where the time goes in v1:
time: 666 us; the launch traced here: 656 us
  local copies, waits for them, and re-layouts  186 us (28%)
  waiting for transfers between devices  124 us (19%)
  matrix products  120 us (18%)
  blocking collectives  119 us (18%)
  other arithmetic  86.8 us (13%)
  between operations  13.8 us (2%)
    all_gather x2, blocking collectives, select_bias(): bias_rowwise = lax.all_gather(bias_part, 'row', axis=0, tiled=True)  119 us
    all_gather x1, waiting for transfers between devices, run_pass(): lax.all_gather(normed, 'col', axis=1, tiled=True)  87.8 us
    dot_general x6, matrix products, accumulate(): jnp.einsum(form, weights.astype(jnp.bfloat16), value_piece, preferred_ele...  52.8 us
    reduce_sum x6, other arithmetic, accumulate(): running_sum = running_sum * factor + jnp.sum(weights, axis=-1)  51.1 us
    all_gather x2, waiting for transfers between devices, select_bias(): full_bias = lax.all_gather(bias_rowwise, 'col', axis=1, tiled=True)  35.3 us
    reshape x6, local copies, waits for them, and re-layouts, attend_ending(): value_four = value_piece.reshape(count, col_count, HEADS, HEAD_DIM)  33.9 us
    reshape x6, local copies, waits for them, and re-layouts, attend_ending(): key_four = key_piece.reshape(count, col_count, HEADS, HEAD_DIM)  33.8 us
    dot_general x3, matrix products, attend_ending(): jnp.einsum('ijhd,kjhd->ijhk', queries, key_four, preferred_element_type=j...  30.3 us
  transfers between devices with their start and end apart: 4, of which 3 were waited for; matrix products, arithmetic and copies ran while one was open for 3% of the time, Pallas kernels for 0%

profile of v1, /device:TPU:0, one launch (start us, length us, event | category | flops | bytes accessed | tf_op | source)
XLA Modules:
  0.0 656.1 jit_solution(2584492703421960636)
XLA Ops:
  13.2 5.3 stack.2
  18.5 5.3 all-to-all-start
  24.5 109.1 %all_gather.15 = bf16[384,96,4]{1,2,0:T(4,128)(2,1)S(1)} all-gather(bf16[48,96,4]{1,2,0:T(4,128)(2,1)S(1)} %copy.62), channel_id=1, replica_groups=mesh['row'=8,'col'=4] {'row'}, dimensions={0}, use_global_device_ids=true | all-gather | bytes 331776 | tf_op jit(solution)/shard_map/all_gather | solution.py:114
  136.1 3.7 copy-done.3
  142.2 5.2 copy.64
  148.2 17.9 %all-gather.4.cloned.1.call-done = bf16[384,384,4]{0,2,1:T(4,128)(2,1)} async-done(((bf16[384,96,4]{0,2,1:T(4,128)(2,1)}), bf16[384,384,4]{0,2,1:T(4,128)(2,1)}) %all-gather.4.cloned.1.call-update) | async-done | bytes 1179664 | tf_op jit(solution)/shard_map/all_gather | solution.py:115
  167.7 207.9 %while.36 = (s32[]{:T(128)}, f32[48,96,4]{0,2,1:T(4,128)}, f32[48,96,4]{0,2,1:T(4,128)}, f32[48,96,4,32]{0,3,2,1:T(8,128)}, s32[384]{0:T(512)S(1)}, /*index=5*/b...) while((s32[]{:T(128)}, f32[48,96,4]{0,2,1:T(4,128)}, ...), condition=%wide.region_5.6_spmd.clone, body=%wide.region_2.5_spmd.clone.sunk | while | flops 1138280576 | bytes 109233432 | solution.py:110
  175.9 3.2 copy.97
  179.1 5.2 reshape.128
  184.2 6.1 copy.98
  191.3 10.1 %fusion.107 = (f32[48,96,4]{0,2,1:T(4,128)}, f32[96,4,128,48]{2,3,1,0:T(8,128)}) fusion(f32[48,4,128]{2,0,1:T(8,128)S(1)} %convert_bitcast_fusion.4, pred[128]{0:T(512)(128)(4,1)S(1)} %dynamic-slice_compare_fusion.4, bf16[128,96,4,32]{0,3,2,1:T(8,128)(2,1)S(1)} %copy.98, bf16[48,96,4,32]{0,3,2,1:T(8,128)(2,1)} %get-tuple-element.672), kind=kOutput, calls=%fused_computation.6.clone.1 | convolution fusion | flops 158054400 | bytes 13934720 | tf_op jit(solution)/shard_map/while/body/eval_jaxpr/ijhd,kjhd->ijhk/dot_general | solution.py:79
  202.4 8.3 %fusion.108 = f32[48,96,4]{0,2,1:T(4,128)S(1)} fusion(f32[96,4,128,48]{2,3,1,0:T(8,128)} %get-tuple-element.620, f32[48,96,4]{0,2,1:T(4,128)S(1)} %select_maximum_fusion.4, f32[48,4,128]{2,0,1:T(8,128)S(1)} %convert_bitcast_fusion.4, pred[128]{0:T(512)(128)(4,1)S(1)} %dynamic-slice_compare_fusion.4), kind=kLoop, calls=%fused_computation.5.clone.1 | loop fusion | flops 9418752 | bytes 9683072 | tf_op jit(solution)/shard_map/while/body/eval_jaxpr/reduce_sum | solution.py:67
  212.4 3.2 copy.99
  215.6 5.2 reshape.129
  220.8 6.1 copy.100
  226.9 8.7 %bitcast_add_fusion.6 = f32[48,96,4,32]{0,3,2,1:T(8,128)} fusion(f32[48,96,4,32]{0,3,2,1:T(8,128)} %get-tuple-element.655, f32[48,96,4]{0,2,1:T(4,128)} %get-tuple-element.622, pred[]{:T(512)S(6)} %compare.6, bf16[128,96,4,32]{0,3,2,1:T(8,128)(2,1)S(1)} %copy.100, f32[96,4,128,48]{2,3,1,0:T(8,128)} %get-tuple-element.620, ...), kind=kOutput, calls=%fused_computation.7.clone.1 | convolution fusion | flops 162201600 | bytes 17547392 | tf_op jit(solution)/shard_map/while/body/eval_jaxpr/ijhk,kjhd->ijhd/dot_general | solution.py:68
  244.0 3.2 copy.97
  247.2 5.2 reshape.128
  252.3 6.1 copy.98
  259.4 10.1 %fusion.107 = (f32[48,96,4]{0,2,1:T(4,128)}, f32[96,4,128,48]{2,3,1,0:T(8,128)}) fusion(f32[48,4,128]{2,0,1:T(8,128)S(1)} %convert_bitcast_fusion.4, pred[128]{0:T(512)(128)(4,1)S(1)} %dynamic-slice_compare_fusion.4, bf16[128,96,4,32]{0,3,2,1:T(8,128)(2,1)S(1)} %copy.98, bf16[48,96,4,32]{0,3,2,1:T(8,128)(2,1)} %get-tuple-element.672), kind=kOutput, calls=%fused_computation.6.clone.1 | convolution fusion | flops 158054400 | bytes 13934720 | tf_op jit(solution)/shard_map/while/body/eval_jaxpr/ijhd,kjhd->ijhk/dot_general | solution.py:79
  270.6 8.3 %fusion.108 = f32[48,96,4]{0,2,1:T(4,128)S(1)} fusion(f32[96,4,128,48]{2,3,1,0:T(8,128)} %get-tuple-element.620, f32[48,96,4]{0,2,1:T(4,128)S(1)} %select_maximum_fusion.4, f32[48,4,128]{2,0,1:T(8,128)S(1)} %convert_bitcast_fusion.4, pred[128]{0:T(512)(128)(4,1)S(1)} %dynamic-slice_compare_fusion.4), kind=kLoop, calls=%fused_computation.5.clone.1 | loop fusion | flops 9418752 | bytes 9683072 | tf_op jit(solution)/shard_map/while/body/eval_jaxpr/reduce_sum | solution.py:67
  280.6 3.2 copy.99
  283.8 5.2 reshape.129
  288.9 6.1 copy.100
  295.1 10.1 %bitcast_add_fusion.6 = f32[48,96,4,32]{0,3,2,1:T(8,128)} fusion(f32[48,96,4,32]{0,3,2,1:T(8,128)} %get-tuple-element.655, f32[48,96,4]{0,2,1:T(4,128)} %get-tuple-element.622, pred[]{:T(512)S(6)} %compare.6, bf16[128,96,4,32]{0,3,2,1:T(8,128)(2,1)S(1)} %copy.100, f32[96,4,128,48]{2,3,1,0:T(8,128)} %get-tuple-element.620, ...), kind=kOutput, calls=%fused_computation.7.clone.1 | convolution fusion | flops 162201600 | bytes 17547392 | tf_op jit(solution)/shard_map/while/body/eval_jaxpr/ijhk,kjhd->ijhd/dot_general | solution.py:68
  316.8 5.2 reshape.128
  321.9 6.1 copy.98
  329.0 10.1 %fusion.107 = (f32[48,96,4]{0,2,1:T(4,128)}, f32[96,4,128,48]{2,3,1,0:T(8,128)}) fusion(f32[48,4,128]{2,0,1:T(8,128)S(1)} %convert_bitcast_fusion.4, pred[128]{0:T(512)(128)(4,1)S(1)} %dynamic-slice_compare_fusion.4, bf16[128,96,4,32]{0,3,2,1:T(8,128)(2,1)S(1)} %copy.98, bf16[48,96,4,32]{0,3,2,1:T(8,128)(2,1)} %get-tuple-element.672), kind=kOutput, calls=%fused_computation.6.clone.1 | convolution fusion | flops 158054400 | bytes 13934720 | tf_op jit(solution)/shard_map/while/body/eval_jaxpr/ijhd,kjhd->ijhk/dot_general | solution.py:79
  340.2 8.3 %fusion.108 = f32[48,96,4]{0,2,1:T(4,128)S(1)} fusion(f32[96,4,128,48]{2,3,1,0:T(8,128)} %get-tuple-element.620, f32[48,96,4]{0,2,1:T(4,128)S(1)} %select_maximum_fusion.4, f32[48,4,128]{2,0,1:T(8,128)S(1)} %convert_bitcast_fusion.4, pred[128]{0:T(512)(128)(4,1)S(1)} %dynamic-slice_compare_fusion.4), kind=kLoop, calls=%fused_computation.5.clone.1 | loop fusion | flops 9418752 | bytes 9683072 | tf_op jit(solution)/shard_map/while/body/eval_jaxpr/reduce_sum | solution.py:67
  353.4 5.2 reshape.129
  358.6 6.1 copy.100
  364.7 10.1 %bitcast_add_fusion.6 = f32[48,96,4,32]{0,3,2,1:T(8,128)} fusion(f32[48,96,4,32]{0,3,2,1:T(8,128)} %get-tuple-element.655, f32[48,96,4]{0,2,1:T(4,128)} %get-tuple-element.622, pred[]{:T(512)S(6)} %compare.6, bf16[128,96,4,32]{0,3,2,1:T(8,128)(2,1)S(1)} %copy.100, f32[96,4,128,48]{2,3,1,0:T(8,128)} %get-tuple-element.620, ...), kind=kOutput, calls=%fused_computation.7.clone.1 | convolution fusion | flops 162201600 | bytes 17547392 | tf_op jit(solution)/shard_map/while/body/eval_jaxpr/ijhk,kjhd->ijhd/dot_general | solution.py:68
  375.6 6.9 %broadcast_divide_fusion = f32[48,96,4,32]{0,3,2,1:T(8,128)} fusion(f32[48,96,4,32]{0,3,2,1:T(8,128)} %get-tuple-element.315, f32[48,96,4]{0,2,1:T(4,128)} %get-tuple-element.316), kind=kLoop, calls=%fused_computation.58 | loop fusion | flops 589824 | bytes 4792320 | tf_op jit(solution)/shard_map/div | solution.py:159
  382.5 5.4 copy.66
  399.9 9.5 %all_gather.18 = bf16[384,96,4]{1,2,0:T(4,128)(2,1)S(1)} all-gather(bf16[48,96,4]{1,2,0:T(4,128)(2,1)S(1)} %copy.69), channel_id=1, replica_groups=mesh['row'=8,'col'=4] {'row'}, dimensions={0}, use_global_device_ids=true | all-gather | bytes 331776 | tf_op jit(solution)/shard_map/all_gather | solution.py:114
  413.8 3.7 copy-done.4
  421.7 17.4 %all-gather.8.cloned.1.call-done = bf16[384,384,4]{0,2,1:T(4,128)(2,1)} async-done(((bf16[384,96,4]{0,2,1:T(4,128)(2,1)}), bf16[384,384,4]{0,2,1:T(4,128)(2,1)}) %all-gather.8.cloned.1.call-update) | async-done | bytes 1179664 | tf_op jit(solution)/shard_map/all_gather | solution.py:115
  441.5 87.8 %all-gather.6.cloned.1.call-done = bf16[48,384,128]{2,1,0:T(8,128)(2,1)} async-done(((bf16[48,96,128]{2,1,0:T(8,128)(2,1)}), bf16[48,384,128]{2,1,0:T(8,128)(2,1)}) %all-gather.6.cloned.1.call-update) | async-done | bytes 4718608 | tf_op jit(solution)/shard_map/all_gather | solution.py:156
  529.4 107.2 %while.37 = (s32[]{:T(128)}, f32[48,96,4]{1,2,0:T(4,128)S(1)}, f32[48,96,4]{1,2,0:T(4,128)}, f32[48,96,4,32]{1,3,2,0:T(8,128)}, s32[384]{0:T(512)S(1)}, /*index=...) while((s32[]{:T(128)}, f32[48,96,4]{1,2,0:T(4,128)S(1)}, ...), condition=%wide.region_11.12_spmd.clone, body=%wide.region_8.11_spmd.clone.sunk | while | flops 734079104 | bytes 90703208 | solution.py:110
  537.3 5.4 fusion.116
  542.7 8.7 %fusion.117 = f32[48,96,4]{1,2,0:T(4,128)S(1)} fusion(f32[48,4,128,96]{2,3,1,0:T(8,128)} %get-tuple-element.635, f32[48,96,4]{1,2,0:T(4,128)S(1)} %select_maximum_fusion.5, f32[96,4,128]{2,0,1:T(8,128)S(1)} %convert_bitcast_fusion.5, pred[128]{0:T(512)(128)(4,1)S(1)} %dynamic-slice_compare_fusion.5), kind=kLoop, calls=%fused_computation.28.clone.1 | loop fusion | flops 9418752 | bytes 9781376 | tf_op jit(solution)/shard_map/while/body/eval_jaxpr/reduce_sum | solution.py:67
  554.8 8.0 %bitcast_add_fusion.7 = f32[48,96,4,32]{1,3,2,0:T(8,128)S(1)} fusion(f32[48,96,4,32]{1,3,2,0:T(8,128)S(1)} %copy-done, f32[48,4,128,96]{2,3,1,0:T(8,128)} %get-tuple-element.635, f32[48,96,4]{1,2,0:T(4,128)S(1)} %select_maximum_fusion.5, f32[96,4,128]{2,0,1:T(8,128)S(1)} %convert_bitcast_fusion.5, ...), kind=kOutput, calls=%fused_computation.36.clone.1 | convolution fusion | flops 162201600 | bytes 16072833 | tf_op jit(solution)/shard_map/while/body/eval_jaxpr/ijhk,ikhd->ijhd/dot_general | solution.py:68
  572.4 5.4 fusion.116
  577.9 8.7 %fusion.117 = f32[48,96,4]{1,2,0:T(4,128)S(1)} fusion(f32[48,4,128,96]{2,3,1,0:T(8,128)} %get-tuple-element.635, f32[48,96,4]{1,2,0:T(4,128)S(1)} %select_maximum_fusion.5, f32[96,4,128]{2,0,1:T(8,128)S(1)} %convert_bitcast_fusion.5, pred[128]{0:T(512)(128)(4,1)S(1)} %dynamic-slice_compare_fusion.5), kind=kLoop, calls=%fused_computation.28.clone.1 | loop fusion | flops 9418752 | bytes 9781376 | tf_op jit(solution)/shard_map/while/body/eval_jaxpr/reduce_sum | solution.py:67
  590.9 8.0 %bitcast_add_fusion.7 = f32[48,96,4,32]{1,3,2,0:T(8,128)S(1)} fusion(f32[48,96,4,32]{1,3,2,0:T(8,128)S(1)} %copy-done, f32[48,4,128,96]{2,3,1,0:T(8,128)} %get-tuple-element.635, f32[48,96,4]{1,2,0:T(4,128)S(1)} %select_maximum_fusion.5, f32[96,4,128]{2,0,1:T(8,128)S(1)} %convert_bitcast_fusion.5, ...), kind=kOutput, calls=%fused_computation.36.clone.1 | convolution fusion | flops 162201600 | bytes 16072833 | tf_op jit(solution)/shard_map/while/body/eval_jaxpr/ijhk,ikhd->ijhd/dot_general | solution.py:68
  608.4 5.4 fusion.116
  613.9 8.7 %fusion.117 = f32[48,96,4]{1,2,0:T(4,128)S(1)} fusion(f32[48,4,128,96]{2,3,1,0:T(8,128)} %get-tuple-element.635, f32[48,96,4]{1,2,0:T(4,128)S(1)} %select_maximum_fusion.5, f32[96,4,128]{2,0,1:T(8,128)S(1)} %convert_bitcast_fusion.5, pred[128]{0:T(512)(128)(4,1)S(1)} %dynamic-slice_compare_fusion.5), kind=kLoop, calls=%fused_computation.28.clone.1 | loop fusion | flops 9418752 | bytes 9781376 | tf_op jit(solution)/shard_map/while/body/eval_jaxpr/reduce_sum | solution.py:67
  626.9 8.0 %bitcast_add_fusion.7 = f32[48,96,4,32]{1,3,2,0:T(8,128)S(1)} fusion(f32[48,96,4,32]{1,3,2,0:T(8,128)S(1)} %copy-done, f32[48,4,128,96]{2,3,1,0:T(8,128)} %get-tuple-element.635, f32[48,96,4]{1,2,0:T(4,128)S(1)} %select_maximum_fusion.5, f32[96,4,128]{2,0,1:T(8,128)S(1)} %convert_bitcast_fusion.5, ...), kind=kOutput, calls=%fused_computation.36.clone.1 | convolution fusion | flops 162201600 | bytes 16072833 | tf_op jit(solution)/shard_map/while/body/eval_jaxpr/ijhk,ikhd->ijhd/dot_general | solution.py:68
  (203 shorter events, 132.9 us)
Async XLA Ops:
  6.5 5.2 copy-start.9
  6.5 4.6 copy-start.23
  18.5 5.4 copy-start.20
  18.5 149.2 %all-to-all-start = ((bf16[8,48,96,128]{3,2,1,0:T(8,128)(2,1)}), bf16[8,48,96,128]{3,2,1,0:T(8,128)(2,1)}, u32[]{:S(2)}, u32[]{:S(2)}) async-start(bf16[8,48,96,128]{3,2,1,0:T(8,128)(2,1)} %stack.2), calls=%async_computation | async-start | bytes 18874368 | tf_op jit(solution)/shard_map/all_to_all | solution.py:14
  23.8 110.9 %copy-start.16 = (bf16[2,128,512]{2,1,0:T(8,128)(2,1)S(1)}, bf16[2,128,512]{2,1,0:T(8,128)(2,1)}, u32[]{:S(2)}) copy-start(bf16[2,128,512]{2,1,0:T(8,128)(2,1)} %param.13) | copy-start | bytes 786436
  23.8 142.2 %all-gather.4.cloned.1.call-start = ((), (), s32[]{:S(2)}) async-start(), calls=%async_computation.1 | async-start | bytes 1474560 | tf_op jit(solution)/shard_map/all_gather | solution.py:115
  134.6 304.5 %all-gather.8.cloned.1.call-start = ((), (), s32[]{:S(2)}) async-start(), calls=%async_computation.3 | async-start | bytes 1474560 | tf_op jit(solution)/shard_map/all_gather | solution.py:115
  136.1 3.7 copy-start.3
  142.2 25.5 %copy-start.24 = (s32[384]{0:T(512)S(1)}, s32[384]{0:T(512)}, u32[]{:S(2)}) copy-start(s32[384]{0:T(512)} %param.11) | copy-start | bytes 4612
  202.4 8.3 %copy-start.6 = (f32[48,96,4]{0,2,1:T(4,128)S(1)}, f32[48,96,4]{0,2,1:T(4,128)}, u32[]{:S(2)}) copy-start(f32[48,96,4]{0,2,1:T(4,128)} %get-tuple-element.653) | copy-start | bytes 221188 | tf_op jit(solution)/shard_map/while
  202.4 8.3 %copy-start.12 = (f32[48,96,4]{0,2,1:T(4,128)S(1)}, f32[48,96,4]{0,2,1:T(4,128)}, u32[]{:S(2)}) copy-start(f32[48,96,4]{0,2,1:T(4,128)} %get-tuple-element.654) | copy-start | bytes 221188 | tf_op jit(solution)/shard_map/while
  211.7 0.7 copy-start.13
  270.6 8.3 %copy-start.6 = (f32[48,96,4]{0,2,1:T(4,128)S(1)}, f32[48,96,4]{0,2,1:T(4,128)}, u32[]{:S(2)}) copy-start(f32[48,96,4]{0,2,1:T(4,128)} %get-tuple-element.653) | copy-start | bytes 221188 | tf_op jit(solution)/shard_map/while
  270.6 8.3 %copy-start.12 = (f32[48,96,4]{0,2,1:T(4,128)S(1)}, f32[48,96,4]{0,2,1:T(4,128)}, u32[]{:S(2)}) copy-start(f32[48,96,4]{0,2,1:T(4,128)} %get-tuple-element.654) | copy-start | bytes 221188 | tf_op jit(solution)/shard_map/while
  279.9 0.7 copy-start.13
  340.2 8.3 %copy-start.6 = (f32[48,96,4]{0,2,1:T(4,128)S(1)}, f32[48,96,4]{0,2,1:T(4,128)}, u32[]{:S(2)}) copy-start(f32[48,96,4]{0,2,1:T(4,128)} %get-tuple-element.653) | copy-start | bytes 221188 | tf_op jit(solution)/shard_map/while
  340.2 8.3 %copy-start.12 = (f32[48,96,4]{0,2,1:T(4,128)S(1)}, f32[48,96,4]{0,2,1:T(4,128)}, u32[]{:S(2)}) copy-start(f32[48,96,4]{0,2,1:T(4,128)} %get-tuple-element.654) | copy-start | bytes 221188 | tf_op jit(solution)/shard_map/while
  349.5 0.7 copy-start.13
  392.6 2.4 copy-start.10
  392.6 2.4 copy-start.18
  395.0 2.8 copy-start.22
  396.1 1.7 copy-start.7
  396.1 3.2 copy-start.21
  399.3 11.2 %copy-start.5 = (bf16[48,96,128]{2,1,0:T(8,128)(2,1)}, bf16[48,96,128]{2,1,0:T(8,128)(2,1)S(1)}, u32[]{:S(2)}) copy-start(bf16[48,96,128]{2,1,0:T(8,128)(2,1)S(1)} %fusion.39) | copy-start | bytes 3538948
  399.3 11.9 %copy-start.17 = (bf16[2,128,512]{2,1,0:T(8,128)(2,1)S(1)}, bf16[2,128,512]{2,1,0:T(8,128)(2,1)}, u32[]{:S(2)}) copy-start(bf16[2,128,512]{2,1,0:T(8,128)(2,1)} %param.13) | copy-start | bytes 786436
  410.4 119.0 %all-gather.6.cloned.1.call-start = ((), (), s32[]{:S(2)}) async-start(), calls=%async_computation.2 | async-start | bytes 5898240 | tf_op jit(solution)/shard_map/all_gather | solution.py:156
  413.8 3.7 copy-start.4
  529.4 13.3 %copy-start.11 = (f32[48,96,4]{1,2,0:T(4,128)}, f32[48,96,4]{1,2,0:T(4,128)S(1)}, u32[]{:S(2)}) copy-start(f32[48,96,4]{1,2,0:T(4,128)S(1)} %get-tuple-element.692) | copy-start | bytes 221188 | tf_op jit(solution)/shard_map/while
  535.8 1.5 copy-start.2
  542.7 8.7 %copy-start.14 = (f32[48,96,4]{1,2,0:T(4,128)S(1)}, f32[48,96,4]{1,2,0:T(4,128)}, u32[]{:S(2)}) copy-start(f32[48,96,4]{1,2,0:T(4,128)} %get-tuple-element.693) | copy-start | bytes 221188 | tf_op jit(solution)/shard_map/while
  551.6 0.6 copy-start.15
  552.9 1.9 copy-start
  562.8 1.7 copy-start.1
  564.5 13.3 %copy-start.11 = (f32[48,96,4]{1,2,0:T(4,128)}, f32[48,96,4]{1,2,0:T(4,128)S(1)}, u32[]{:S(2)}) copy-start(f32[48,96,4]{1,2,0:T(4,128)S(1)} %get-tuple-element.692) | copy-start | bytes 221188 | tf_op jit(solution)/shard_map/while
  570.9 1.5 copy-start.2
  577.8 8.7 %copy-start.14 = (f32[48,96,4]{1,2,0:T(4,128)S(1)}, f32[48,96,4]{1,2,0:T(4,128)}, u32[]{:S(2)}) copy-start(f32[48,96,4]{1,2,0:T(4,128)} %get-tuple-element.693) | copy-start | bytes 221188 | tf_op jit(solution)/shard_map/while
  587.6 0.6 copy-start.15
  589.0 1.9 copy-start
  598.8 1.7 copy-start.1
  600.5 13.3 %copy-start.11 = (f32[48,96,4]{1,2,0:T(4,128)}, f32[48,96,4]{1,2,0:T(4,128)S(1)}, u32[]{:S(2)}) copy-start(f32[48,96,4]{1,2,0:T(4,128)S(1)} %get-tuple-element.692) | copy-start | bytes 221188 | tf_op jit(solution)/shard_map/while
  607.0 1.5 copy-start.2
  613.9 8.7 %copy-start.14 = (f32[48,96,4]{1,2,0:T(4,128)S(1)}, f32[48,96,4]{1,2,0:T(4,128)}, u32[]{:S(2)}) copy-start(f32[48,96,4]{1,2,0:T(4,128)} %get-tuple-element.693) | copy-start | bytes 221188 | tf_op jit(solution)/shard_map/while
  623.7 0.6 copy-start.15
  625.0 1.9 copy-start
  634.9 1.7 copy-start.1
  645.5 2.4 copy-start.8
  645.5 2.4 copy-start.19
Sparse Core Ops, SparseCore 0:
  134.7 31.3 all-gather.3
  410.5 28.5 all-gather.7
  440.7 88.6 all-gather.5
